TPU v7x, 32 devices: a whole 2x2x4 slice. The times are simulated.
32 devices in a mesh: dp: 4 (over y, x), head: 8 (over z, core).
Axes of the slice: x: 2, y: 2, z: 4, core: 2. Of those that a mesh axis runs over, the one named last changes fastest.
Arguments:
- latents: bfloat16 [512, 512], P('dp'), may hold values from -6 to 6
- targets: bfloat16 [512, 32768], P('dp', 'head'), may hold values from -6 to 6
- kv_weight: bfloat16 [512, 32768], P(None, 'head'), may hold values from -0.25 to 0.25
- momentum: float32 [512, 8, 4096], P(None, 'head', 'dp'), may hold values from -120 to 120
Outputs:
- momentum_out: float32 [512, 8, 4096], P(None, 'head', 'dp')
- update: float32 [512, 8, 4096], P(None, 'head', 'dp')
All inputs are finite; a program needn't handle non-finite values.
Results may differ from a plain program's by a relative error of at most 0.0003.
The roundings to bfloat16 on the way count: a program that leaves them out, or rounds other values in their place, can miss the bound.
Values may be sent and summed in bfloat16 or wider, within the bound.
No kernel may reach another device: no remote copies, remote signals or barrier semaphores. Data moves between devices by JAX's collectives and lax.ppermute only.
A program may use at most 64 MiB of HBM per device.

v0:
```python
import functools
import math

import jax
import jax.numpy as jnp
from jax import lax
from jax.experimental import pallas as pl
from jax.experimental.pallas import tpu as pltpu
from jax.sharding import PartitionSpec as P


LANES = 128

decay_rate = 0.95
linear_coef = 3.4445
square_coef = -4.775
quint_coef = 2.0315
epsilon = 1e-07
iterations = 2


ROWS_BY_ROWS = (((1,), (1,)), ((), ()))


def split(value):
    high = value.astype(jnp.bfloat16)
    low = (value - high.astype(jnp.float32)).astype(jnp.bfloat16)
    return high, low


def dot(left, right, dims=(((1,), (0,)), ((), ()))):
    return lax.dot_general(left, right, dims, preferred_element_type=jnp.float32)


def product(left, right):
    left_high, left_low = split(left)
    right_high, right_low = split(right)
    return (
        dot(left_high, right_low) + dot(left_low, right_high) + dot(left_high, right_high)
    )


def swap(value, axis, mask):
    size = lax.axis_size(axis)
    return lax.ppermute(value, axis, [(i, i ^ mask) for i in range(size)])


def pick(stack, index):
    return lax.dynamic_index_in_dim(stack, index, 0, keepdims=False)


def few(size):
    return size in (2, 4)


def scatter_sum(value, axis):
    size = lax.axis_size(axis)
    parts = value.reshape(size, value.shape[0] // size, *value.shape[1:])
    if not few(size):
        return jnp.sum(lax.all_to_all(parts, axis, 0, 0), axis=0)
    me = lax.axis_index(axis)
    arrived = [swap(pick(parts, me ^ mask), axis, mask) for mask in range(1, size)]
    total = pick(parts, me)
    for part in arrived:
        total = total + part
    return total


def gather(value, axis):
    size = lax.axis_size(axis)
    if not few(size):
        return lax.all_gather(value, axis, axis=0, tiled=True)
    me = lax.axis_index(axis)
    parts = jnp.stack([value] + [swap(value, axis, mask) for mask in range(1, size)])
    return jnp.concatenate([pick(parts, me ^ owner) for owner in range(size)], axis=0)


def sum_over_devices(packed):
    heads = lax.axis_size("head")
    core = lax.axis_index("head") % 2
    halves = packed.reshape(2, packed.shape[0] // 2, *packed.shape[1:])
    half = pick(halves, core) + swap(pick(halves, 1 - core), "head", 1)
    part = scatter_sum(half, "dp")
    if heads == 8:
        arrived = [swap(part, "head", 2 * mask) for mask in range(1, 4)]
        part = (part + arrived[0]) + (arrived[1] + arrived[2])
    else:
        mask = 2
        while mask < heads:
            part = part + swap(part, "head", mask)
            mask *= 2
    half = gather(part, "dp")
    other = swap(half, "head", 1)
    return jnp.concatenate(
        [jnp.where(core == 0, half, other), jnp.where(core == 0, other, half)], axis=0
    )


def tile_rows(i, j, tiles):
    return pl.ds(i * 8 * tiles + j, 8, stride=tiles)


def front_kernel(arrivals, tiles, scale, *refs):
    (lat_ref, lat_t_ref, weight_ref), refs = refs[:3], refs[3:]
    wanted_refs, refs = refs[:arrivals], refs[arrivals:]
    (targets_ref, momentum_ref, momentum_out_ref, packed_ref), refs = refs[:4], refs[4:]
    high_out_ref, low_out_ref, mine, old, new, residual, nesterov, high_ref, low_ref, sems = refs
    rows, width = nesterov.shape
    load = pltpu.make_async_copy(momentum_ref, old, sems.at[0])
    arrived = sum(wanted_ref.shape[0] for wanted_ref in wanted_refs)
    if arrived < lat_ref.shape[0]:
        first = pl.multiple_of(lax.axis_index("dp") * width, width)
        own = pltpu.make_async_copy(targets_ref.at[:, pl.ds(first, width)], mine, sems.at[1])
        own.start()
        wanted_refs = (*wanted_refs, mine)
    load.start()
    predicted = dot(lat_ref[...], weight_ref[...])
    start = 0
    for wanted_ref in wanted_refs:
        if start == arrived:
            own.wait()
        count = wanted_ref.shape[0]
        residual[pl.ds(start, count), :] = (
            predicted[start : start + count] - wanted_ref[...].astype(jnp.float32)
        ).astype(jnp.bfloat16)
        start += count
    nesterov[...] = dot(lat_t_ref[...], residual[...])
    load.wait()
    for i in range(rows // 8):
        for j in range(tiles):
            here = (pl.ds(i * 8, 8), pl.ds(j * LANES, LANES))
            gradient = nesterov[here] * scale
            fresh = decay_rate * old[tile_rows(i, j, tiles), :] + gradient
            new[tile_rows(i, j, tiles), :] = fresh
            nesterov[here] = gradient + decay_rate * fresh
    high, low = split(nesterov[...])
    high_ref[...] = high
    low_ref[...] = low
    stores = [
        pltpu.make_async_copy(new, momentum_out_ref, sems.at[0]),
        pltpu.make_async_copy(high_ref, high_out_ref, sems.at[1]),
        pltpu.make_async_copy(low_ref, low_out_ref, sems.at[2]),
    ]
    for store in stores:
        store.start()
    blocks = rows // LANES
    slot = 0
    for i in range(blocks):
        strip = pl.ds(i * LANES, LANES)
        after = pl.ds(i * LANES, (blocks - i) * LANES)
        gram = (
            dot(high_ref[strip, :], low_ref[after, :], ROWS_BY_ROWS)
            + dot(low_ref[strip, :], high_ref[after, :], ROWS_BY_ROWS)
            + dot(high_ref[strip, :], high_ref[after, :], ROWS_BY_ROWS)
        )
        for j in range(blocks - i):
            packed_ref[pl.ds(slot * LANES, LANES), :] = gram[:, j * LANES : (j + 1) * LANES]
            slot += 1
    for store in stores:
        store.wait()


def in_hbm(array):
    return pltpu.with_memory_space_constraint(array, pltpu.HBM)


def front(lat, weight, wanted, targets, momentum, scale):
    rows, width = weight.shape
    blocks, tiles = rows // LANES, width // LANES
    count = blocks * (blocks + 1) // 2
    vmem = pl.BlockSpec(memory_space=pltpu.VMEM)
    hbm = pl.BlockSpec(memory_space=pl.ANY)
    half = pltpu.HBM((rows, width), jnp.bfloat16)
    linear = (rows * tiles, LANES)
    return pl.pallas_call(
        functools.partial(front_kernel, len(wanted), tiles, scale),
        out_shape=(
            pltpu.HBM(linear, jnp.float32),
            jax.ShapeDtypeStruct((count * LANES, LANES), jnp.float32),
            half,
            half,
        ),
        in_specs=[vmem] * (3 + len(wanted)) + [hbm, hbm],
        out_specs=(hbm, vmem, hbm, hbm),
        scratch_shapes=[
            pltpu.VMEM((targets.shape[0], width), targets.dtype),
            pltpu.VMEM(linear, jnp.float32),
            pltpu.VMEM(linear, jnp.float32),
            pltpu.VMEM((lat.shape[0], width), jnp.bfloat16),
            pltpu.VMEM((rows, width), jnp.float32),
            pltpu.VMEM((rows, width), jnp.bfloat16),
            pltpu.VMEM((rows, width), jnp.bfloat16),
            pltpu.SemaphoreType.DMA((3,)),
        ],
        compiler_params=pltpu.CompilerParams(vmem_limit_bytes=28 << 20),
        name="front",
    )(lat, lat.T, weight, *wanted, in_hbm(targets), in_hbm(momentum.reshape(linear)))


def finish_kernel(
    tiles, scale, packed_ref, high_hbm, low_hbm, out_hbm, gram_ref, high_ref, low_ref, result, out, sems
):
    loads = [
        pltpu.make_async_copy(high_hbm, high_ref, sems.at[0]),
        pltpu.make_async_copy(low_hbm, low_ref, sems.at[1]),
    ]
    for load in loads:
        load.start()
    rows = gram_ref.shape[0]
    blocks = rows // LANES
    slot = 0
    for i in range(blocks):
        for j in range(i, blocks):
            block = packed_ref[pl.ds(slot * LANES, LANES), :]
            gram_ref[pl.ds(i * LANES, LANES), pl.ds(j * LANES, LANES)] = block
            if j > i:
                gram_ref[pl.ds(j * LANES, LANES), pl.ds(i * LANES, LANES)] = block.T
            slot += 1
    gram = gram_ref[...]
    row = lax.broadcasted_iota(jnp.int32, gram.shape, 0)
    column = lax.broadcasted_iota(jnp.int32, gram.shape, 1)
    diagonal = row == column
    squares = jnp.sum(jnp.where(diagonal, gram, 0.0), keepdims=True)
    inverse = 1.0 / (jnp.sqrt(squares) + epsilon)
    gram = (gram * inverse) * inverse
    identity = jnp.where(diagonal, linear_coef, 0.0)
    total = None
    for iteration in range(iterations):
        factor = identity + square_coef * gram + quint_coef * product(gram, gram)
        total = factor if total is None else product(factor, total)
        if iteration + 1 < iterations:
            gram = product(product(gram, factor), factor)
    left_high, left_low = split(total * (inverse * scale))
    for load in loads:
        load.wait()
    step = rows // 2
    stores = []
    for part in range(2):
        here = slice(part * step, (part + 1) * step)
        result[...] = (
            dot(left_high[here], low_ref[...])
            + dot(left_low[here], high_ref[...])
            + dot(left_high[here], high_ref[...])
        )
        for i in range(step // 8):
            for j in range(tiles):
                out[tile_rows(part * step // 8 + i, j, tiles), :] = result[
                    pl.ds(i * 8, 8), pl.ds(j * LANES, LANES)
                ]
        chunk = pl.ds(part * step * tiles, step * tiles)
        store = pltpu.make_async_copy(out.at[chunk, :], out_hbm.at[chunk, :], sems.at[2 + part])
        store.start()
        stores.append(store)
    for store in stores:
        store.wait()


def finish(packed, high, low, scale):
    rows, width = high.shape
    tiles = width // LANES
    linear = (rows * tiles, LANES)
    vmem = pl.BlockSpec(memory_space=pltpu.VMEM)
    hbm = pl.BlockSpec(memory_space=pl.ANY)
    return pl.pallas_call(
        functools.partial(finish_kernel, tiles, scale),
        out_shape=pltpu.HBM(linear, jnp.float32),
        in_specs=[vmem, hbm, hbm],
        out_specs=hbm,
        scratch_shapes=[
            pltpu.VMEM((rows, rows), jnp.float32),
            pltpu.VMEM((rows, width), jnp.bfloat16),
            pltpu.VMEM((rows, width), jnp.bfloat16),
            pltpu.VMEM((rows // 2, width), jnp.float32),
            pltpu.VMEM(linear, jnp.float32),
            pltpu.SemaphoreType.DMA((4,)),
        ],
        compiler_params=pltpu.CompilerParams(vmem_limit_bytes=28 << 20),
        name="finish",
    )(packed, in_hbm(high), in_hbm(low))


def columns_of(array, index, width):
    return lax.dynamic_slice_in_dim(array, index * width, width, axis=1)


def gather_tokens(latents, targets, width):
    groups = lax.axis_size("dp")
    if not few(groups):
        lat = lax.all_gather(latents, "dp", axis=0, tiled=True)
        wanted = lax.all_to_all(targets, "dp", split_axis=1, concat_axis=0, tiled=True)
        return lat, [wanted]
    me = lax.axis_index("dp")
    core = lax.axis_index("head") % 2
    tokens, rows = latents.shape
    mine = pick(latents.reshape(2, tokens // 2, rows), core)
    wanted = [columns_of(targets, me ^ mask, width) for mask in range(1, groups)]
    first = []
    for mask in range(1, groups):
        first.append(swap(mine, "dp", mask))
    first = jnp.stack(first)
    second = swap(first, "head", 1)
    others = jnp.stack(
        [jnp.where(core == 0, first, second), jnp.where(core == 0, second, first)], axis=1
    )
    lat = jnp.concatenate([others.reshape((groups - 1) * tokens, rows), latents], axis=0)
    arrived = []
    for mask in range(1, groups):
        arrived.append(swap(wanted[mask - 1], "dp", mask))
    return lat, arrived


def local(total_columns, latents, targets, kv_weight, momentum):
    rows = momentum.shape[0]
    width = momentum.shape[2]
    weight = columns_of(kv_weight, lax.axis_index("dp"), width)
    lat, wanted = gather_tokens(latents, targets, width)
    momentum_new, packed, high, low = front(
        lat, weight, wanted, targets, momentum, 1.0 / math.sqrt(lat.shape[0])
    )
    packed = sum_over_devices(packed)
    update = finish(packed, high, low, math.sqrt(total_columns))
    return momentum_new.reshape(rows, 1, width), update.reshape(rows, 1, width)


def solution(mesh):

    def step(latents, targets, kv_weight, momentum):
        total_columns = kv_weight.shape[1]
        return jax.shard_map(
            functools.partial(local, total_columns),
            mesh=mesh,
            in_specs=(P("dp", None), P("dp", "head"), P(None, "head"), P(None, "head", "dp")),
            out_specs=(P(None, "head", "dp"), P(None, "head", "dp")),
            check_vma=False,
        )(latents, targets, kv_weight, momentum)

    return step
```

profile of v0, /device:TPU:0, one launch (start us, length us, event | category | flops | bytes accessed | tf_op | source)
XLA Modules:
  0.0 70.2 jit_solution(17061686711524027830)
XLA Ops:
  0.6 0.0 copy-start
  0.7 0.9 %dynamic-slice_bitcast_fusion.8 = bf16[64,512]{1,0:T(8,128)(2,1)S(1)} fusion(bf16[2,64,512]{2,1,0:T(8,128)(2,1)} %bitcast.54, s32[]{:T(128)S(6)} %select_n.73), kind=kLoop, calls=%fused_computation.23 | loop fusion | bytes 131076 | tf_op jit(solution)/shard_map/jit(dynamic_index_in_dim)/squeeze | solution.py:49
  1.5 3.9 %collective-permute-start.2 = (bf16[64,512]{1,0:T(8,128)(2,1)S(1)}, bf16[64,512]{1,0:T(8,128)(2,1)S(1)}, u32[]{:S(2)}, u32[]{:S(2)}) collective-permute-start(bf16[64,512]{1,0:T(8,128)(2,1)S(1)} %dynamic-slice_bitcast_fusion.8), channel_id=1, source_target_pairs={{0,24},{8,16},{16,8},{24,0},{1,25},{9,17},{17,9},{25,1},{2,26},{10... | collective-permute-start | bytes 196616 | tf_op jit(solution)/shard_map/ppermute | solution.py:45
  5.5 0.5 collective-permute-start.1
  6.0 0.1 collective-permute-start
  6.0 1.7 %collective-permute-done.2 = bf16[64,512]{1,0:T(8,128)(2,1)S(1)} collective-permute-done((bf16[64,512]{1,0:T(8,128)(2,1)S(1)}, bf16[64,512]{1,0:T(8,128)(2,1)S(1)}, u32[]{:S(2)}, u32[]{:S(2)}) %collective-permute-start.2) | collective-permute-done | bytes 65568 | tf_op jit(solution)/shard_map/ppermute | solution.py:45
  7.7 2.0 %collective-permute-done.1 = bf16[64,512]{1,0:T(8,128)(2,1)S(1)} collective-permute-done((bf16[64,512]{1,0:T(8,128)(2,1)S(1)}, bf16[64,512]{1,0:T(8,128)(2,1)S(1)}, u32[]{:S(2)}, u32[]{:S(2)}) %collective-permute-start.1) | collective-permute-done | bytes 65568 | tf_op jit(solution)/shard_map/ppermute | solution.py:45
  9.7 0.5 collective-permute-done
  10.3 0.1 collective-permute-start.3
  10.4 2.0 %constant_dynamic-slice_fusion = (bf16[128,1024]{1,0:T(8,128)(2,1)}, bf16[128,1024]{1,0:T(8,128)(2,1)}, bf16[128,1024]{1,0:T(8,128)(2,1)}) fusion(bf16[128,4096]{1,0:T(8,128)(2,1)} %refs_6_.1, s32[]{:T(128)S(6)} %select_n.79, s32[]{:T(128)S(6)} %select_n.78, s32[]{:T(128)S(6)} %select_n.77), kind=kLoop, calls=%fused_computation.24 | loop fusion | bytes 1572876 | tf_op jit(solution)/shard_map/dynamic_slice | solution.py:283
  12.4 1.5 %collective-permute-start.6 = (bf16[128,1024]{1,0:T(8,128)(2,1)}, bf16[128,1024]{1,0:T(8,128)(2,1)S(1)}, u32[]{:S(2)}, u32[]{:S(2)}) collective-permute-start(bf16[128,1024]{1,0:T(8,128)(2,1)} %get-tuple-element.14), channel_id=1, source_target_pairs={{0,24},{8,16},{16,8},{24,0},{1,25},{9,17},{17,9},{25,1},{2,26},{10... | collective-permute-start | bytes 786440 | tf_op jit(solution)/shard_map/ppermute | solution.py:45
  13.9 0.4 collective-permute-start.5
  14.3 1.6 %collective-permute-start.4 = (bf16[128,1024]{1,0:T(8,128)(2,1)}, bf16[128,1024]{1,0:T(8,128)(2,1)S(1)}, u32[]{:S(2)}, u32[]{:S(2)}) collective-permute-start(bf16[128,1024]{1,0:T(8,128)(2,1)} %get-tuple-element.16), channel_id=1, source_target_pairs={{0,8},{8,0},{16,24},{24,16},{1,9},{9,1},{17,25},{25,17},{2,10},{10... | collective-permute-start | bytes 786440 | tf_op jit(solution)/shard_map/ppermute | solution.py:45
  15.9 0.0 copy-done
  15.9 0.1 copy.16
  16.0 1.3 %constant_dynamic-slice_fusion.3.refs_2_ = bf16[512,1024]{1,0:T(8,128)(2,1)S(1)} fusion(bf16[512,4096]{1,0:T(8,128)(2,1)} %param.6, s32[]{:T(128)S(6)} %select_n.76), kind=kLoop, calls=%fused_computation.27 | loop fusion | bytes 2097156 | tf_op jit(solution)/shard_map/dynamic_slice | solution.py:283
  17.3 0.0 collective-permute-done.3
  17.4 0.2 copy.15
  17.6 0.1 fusion.2
  17.7 0.2 copy.17.refs_0_
  17.9 4.8 %collective-permute-done.6.refs_5_ = bf16[128,1024]{1,0:T(8,128)(2,1)S(1)} collective-permute-done((bf16[128,1024]{1,0:T(8,128)(2,1)}, bf16[128,1024]{1,0:T(8,128)(2,1)S(1)}, u32[]{:S(2)}, u32[]{:S(2)}) %collective-permute-start.6) | collective-permute-done | bytes 262176 | tf_op jit(solution)/shard_map/ppermute | solution.py:45
  22.7 5.1 %collective-permute-done.5.refs_4_ = bf16[128,1024]{1,0:T(8,128)(2,1)S(1)} collective-permute-done((bf16[128,1024]{1,0:T(8,128)(2,1)}, bf16[128,1024]{1,0:T(8,128)(2,1)S(1)}, u32[]{:S(2)}, u32[]{:S(2)}) %collective-permute-start.5) | collective-permute-done | bytes 262176 | tf_op jit(solution)/shard_map/ppermute | solution.py:45
  27.8 0.1 collective-permute-done.4.refs_3_
  27.9 5.5 %front.1 = (f32[4096,128]{1,0:T(8,128)}, f32[1280,128]{1,0:T(8,128)S(1)}, bf16[512,1024]{1,0:T(8,128)(2,1)}, bf16[512,1024]{1,0:T(8,128)(2,1)}) custom-call(bf16[512,512]{1,0:T(8,128)(2,1)S(1)} %copy.17.refs_0_, bf16[512,512]{1,0:T(8,128)(2,1)S(1)} %get-tuple-element.19.refs_1_, bf16[512,1024]{1,0:T(8,128)(2,1)S(1)} %constant_dynamic-slice_fusion.3.refs_2_, ...), custom_call_target="tpu_custom_call" | custom-call | tf_op jit(solution)/shard_map/front/pallas_call | solution.py:175
  33.5 0.1 collective-permute-start.7
  33.6 1.6 %collective-permute-done.7 = f32[640,128]{1,0:T(8,128)S(1)} collective-permute-done((f32[640,128]{1,0:T(8,128)S(1)}, f32[640,128]{1,0:T(8,128)S(1)}, u32[]{:S(2)}, u32[]{:S(2)}) %collective-permute-start.7) | collective-permute-done | bytes 327712 | tf_op jit(solution)/shard_map/ppermute | solution.py:45
  35.3 0.6 collective-permute-start.8
  35.9 1.6 %collective-permute-start.10 = (f32[160,128]{1,0:T(8,128)S(1)}, f32[160,128]{1,0:T(8,128)S(1)}, u32[]{:S(2)}, u32[]{:S(2)}) collective-permute-start(f32[160,128]{1,0:T(8,128)S(1)} %get-tuple-element.28), channel_id=1, source_target_pairs={{0,24},{8,16},{16,8},{24,0},{1,25},{9,17},{17,9},{25,1},{2,26},{10... | collective-permute-start | bytes 245768 | tf_op jit(solution)/shard_map/ppermute | solution.py:45
  37.4 1.4 %collective-permute-start.9 = (f32[160,128]{1,0:T(8,128)S(1)}, f32[160,128]{1,0:T(8,128)S(1)}, u32[]{:S(2)}, u32[]{:S(2)}) collective-permute-start(f32[160,128]{1,0:T(8,128)S(1)} %get-tuple-element.29), channel_id=1, source_target_pairs={{0,16},{8,24},{16,0},{24,8},{1,17},{9,25},{17,1},{25,9},{2,18},{10... | collective-permute-start | bytes 245768 | tf_op jit(solution)/shard_map/ppermute | solution.py:45
  38.8 1.6 %collective-permute-done.8 = f32[160,128]{1,0:T(8,128)S(1)} collective-permute-done((f32[160,128]{1,0:T(8,128)S(1)}, f32[160,128]{1,0:T(8,128)S(1)}, u32[]{:S(2)}, u32[]{:S(2)}) %collective-permute-start.8) | collective-permute-done | bytes 81952 | tf_op jit(solution)/shard_map/ppermute | solution.py:45
  40.4 1.3 %collective-permute-done.10 = f32[160,128]{1,0:T(8,128)S(1)} collective-permute-done((f32[160,128]{1,0:T(8,128)S(1)}, f32[160,128]{1,0:T(8,128)S(1)}, u32[]{:S(2)}, u32[]{:S(2)}) %collective-permute-start.10) | collective-permute-done | bytes 81952 | tf_op jit(solution)/shard_map/ppermute | solution.py:45
  41.7 1.2 %collective-permute-done.9 = f32[160,128]{1,0:T(8,128)S(1)} collective-permute-done((f32[160,128]{1,0:T(8,128)S(1)}, f32[160,128]{1,0:T(8,128)S(1)}, u32[]{:S(2)}, u32[]{:S(2)}) %collective-permute-start.9) | collective-permute-done | bytes 81952 | tf_op jit(solution)/shard_map/ppermute | solution.py:45
  42.9 3.7 %collective-permute-start.13 = (f32[160,128]{1,0:T(8,128)S(1)}, f32[160,128]{1,0:T(8,128)S(1)}, u32[]{:S(2)}, u32[]{:S(2)}) collective-permute-start(f32[160,128]{1,0:T(8,128)S(1)} %fusion.1), channel_id=1, source_target_pairs={{0,6},{1,7},{2,4},{3,5},{4,2},{5,3},{6,0},{7,1},{8,14},{9,15},{10,... | collective-permute-start | bytes 245768 | tf_op jit(solution)/shard_map/ppermute | solution.py:45
  46.6 0.0 collective-permute-start.12
  46.6 0.7 %collective-permute-start.11 = (f32[160,128]{1,0:T(8,128)S(1)}, f32[160,128]{1,0:T(8,128)S(1)}, u32[]{:S(2)}, u32[]{:S(2)}) collective-permute-start(f32[160,128]{1,0:T(8,128)S(1)} %fusion.1), channel_id=1, source_target_pairs={{0,2},{1,3},{2,0},{3,1},{4,6},{5,7},{6,4},{7,5},{8,10},{9,11},{10,... | collective-permute-start | bytes 245768 | tf_op jit(solution)/shard_map/ppermute | solution.py:45
  47.4 2.8 %collective-permute-done.13 = f32[160,128]{1,0:T(8,128)S(1)} collective-permute-done((f32[160,128]{1,0:T(8,128)S(1)}, f32[160,128]{1,0:T(8,128)S(1)}, u32[]{:S(2)}, u32[]{:S(2)}) %collective-permute-start.13) | collective-permute-done | bytes 81952 | tf_op jit(solution)/shard_map/ppermute | solution.py:45
  50.2 3.0 %collective-permute-done.12 = f32[160,128]{1,0:T(8,128)S(1)} collective-permute-done((f32[160,128]{1,0:T(8,128)S(1)}, f32[160,128]{1,0:T(8,128)S(1)}, u32[]{:S(2)}, u32[]{:S(2)}) %collective-permute-start.12) | collective-permute-done | bytes 81952 | tf_op jit(solution)/shard_map/ppermute | solution.py:45
  53.1 0.0 collective-permute-done.11
  53.2 1.7 %collective-permute-start.16 = (f32[160,128]{1,0:T(8,128)S(1)}, f32[160,128]{1,0:T(8,128)S(1)}, u32[]{:S(2)}, u32[]{:S(2)}) collective-permute-start(f32[160,128]{1,0:T(8,128)S(1)} %add_add_fusion), channel_id=1, source_target_pairs={{0,24},{8,16},{16,8},{24,0},{1,25},{9,17},{17,9},{25,1},{2,26},{10... | collective-permute-start | bytes 245768 | tf_op jit(solution)/shard_map/ppermute | solution.py:45
  54.9 1.3 %collective-permute-start.15 = (f32[160,128]{1,0:T(8,128)S(1)}, f32[160,128]{1,0:T(8,128)S(1)}, u32[]{:S(2)}, u32[]{:S(2)}) collective-permute-start(f32[160,128]{1,0:T(8,128)S(1)} %add_add_fusion), channel_id=1, source_target_pairs={{0,16},{8,24},{16,0},{24,8},{1,17},{9,25},{17,1},{25,9},{2,18},{10... | collective-permute-start | bytes 245768 | tf_op jit(solution)/shard_map/ppermute | solution.py:45
  56.2 0.5 collective-permute-start.14
  56.7 2.5 %collective-permute-done.16 = f32[160,128]{1,0:T(8,128)S(1)} collective-permute-done((f32[160,128]{1,0:T(8,128)S(1)}, f32[160,128]{1,0:T(8,128)S(1)}, u32[]{:S(2)}, u32[]{:S(2)}) %collective-permute-start.16) | collective-permute-done | bytes 81952 | tf_op jit(solution)/shard_map/ppermute | solution.py:45
  59.2 0.7 collective-permute-done.15
  59.9 0.7 %collective-permute-done.14 = f32[160,128]{1,0:T(8,128)S(1)} collective-permute-done((f32[160,128]{1,0:T(8,128)S(1)}, f32[160,128]{1,0:T(8,128)S(1)}, u32[]{:S(2)}, u32[]{:S(2)}) %collective-permute-start.14) | collective-permute-done | bytes 81952 | tf_op jit(solution)/shard_map/ppermute | solution.py:45
  60.7 0.1 collective-permute-start.17
  60.8 1.6 %collective-permute-done.17 = f32[640,128]{1,0:T(8,128)S(1)} collective-permute-done((f32[640,128]{1,0:T(8,128)S(1)}, f32[640,128]{1,0:T(8,128)S(1)}, u32[]{:S(2)}, u32[]{:S(2)}) %collective-permute-start.17) | collective-permute-done | bytes 327712 | tf_op jit(solution)/shard_map/ppermute | solution.py:45
  62.5 7.7 %finish.1 = f32[4096,128]{1,0:T(8,128)} custom-call(f32[1280,128]{1,0:T(8,128)S(1)} %pad_maximum_fusion.packed_ref, bf16[512,1024]{1,0:T(8,128)(2,1)} %get-tuple-element.8.high_hbm, bf16[512,1024]{1,0:T(8,128)(2,1)} %get-tuple-element.9.low_hbm), custom_call_target="tpu_custom_call" | custom-call | tf_op jit(solution)/shard_map/finish/pallas_call | solution.py:264
  (14 shorter events, 0.4 us)
Async XLA Ops:
  0.6 15.2 %copy-start = (bf16[128,512]{1,0:T(8,128)(2,1)S(1)}, bf16[128,512]{1,0:T(8,128)(2,1)}, u32[]{:S(2)}) copy-start(bf16[128,512]{1,0:T(8,128)(2,1)} %param.4) | copy-start | bytes 393220
  1.5 6.2 %collective-permute-start.2 = (bf16[64,512]{1,0:T(8,128)(2,1)S(1)}, bf16[64,512]{1,0:T(8,128)(2,1)S(1)}, u32[]{:S(2)}, u32[]{:S(2)}) collective-permute-start(bf16[64,512]{1,0:T(8,128)(2,1)S(1)} %dynamic-slice_bitcast_fusion.8), channel_id=1, source_target_pairs={{0,24},{8,16},{16,8},{24,0},{1,25},{9,17},{17,9},{25,1},{2,26},{10... | collective-permute-start | bytes 196616 | tf_op jit(solution)/shard_map/ppermute | solution.py:45
  5.5 4.3 %collective-permute-start.1 = (bf16[64,512]{1,0:T(8,128)(2,1)S(1)}, bf16[64,512]{1,0:T(8,128)(2,1)S(1)}, u32[]{:S(2)}, u32[]{:S(2)}) collective-permute-start(bf16[64,512]{1,0:T(8,128)(2,1)S(1)} %dynamic-slice_bitcast_fusion.8), channel_id=1, source_target_pairs={{0,16},{8,24},{16,0},{24,8},{1,17},{9,25},{17,1},{25,9},{2,18},{10... | collective-permute-start | bytes 196616 | tf_op jit(solution)/shard_map/ppermute | solution.py:45
  6.0 4.3 %collective-permute-start = (bf16[64,512]{1,0:T(8,128)(2,1)S(1)}, bf16[64,512]{1,0:T(8,128)(2,1)S(1)}, u32[]{:S(2)}, u32[]{:S(2)}) collective-permute-start(bf16[64,512]{1,0:T(8,128)(2,1)S(1)} %dynamic-slice_bitcast_fusion.8), channel_id=1, source_target_pairs={{0,8},{8,0},{16,24},{24,16},{1,9},{9,1},{17,25},{25,17},{2,10},{10... | collective-permute-start | bytes 196616 | tf_op jit(solution)/shard_map/ppermute | solution.py:45
  10.3 7.0 %collective-permute-start.3 = (bf16[3,64,512]{2,1,0:T(8,128)(2,1)S(1)}, bf16[3,64,512]{2,1,0:T(8,128)(2,1)S(1)}, u32[]{:S(2)}, u32[]{:S(2)}) collective-permute-start(bf16[3,64,512]{2,1,0:T(8,128)(2,1)S(1)} %pad_maximum_fusion.5), channel_id=1, source_target_pairs={{0,1},{1,0},{2,3},{3,2},{4,5},{5,4},{6,7},{7,6},{8,9},{9,8},{10,11... | collective-permute-start | bytes 589832 | tf_op jit(solution)/shard_map/ppermute | solution.py:45
  12.4 10.3 %collective-permute-start.6 = (bf16[128,1024]{1,0:T(8,128)(2,1)}, bf16[128,1024]{1,0:T(8,128)(2,1)S(1)}, u32[]{:S(2)}, u32[]{:S(2)}) collective-permute-start(bf16[128,1024]{1,0:T(8,128)(2,1)} %get-tuple-element.14), channel_id=1, source_target_pairs={{0,24},{8,16},{16,8},{24,0},{1,25},{9,17},{17,9},{25,1},{2,26},{10... | collective-permute-start | bytes 786440 | tf_op jit(solution)/shard_map/ppermute | solution.py:45
  13.9 13.9 %collective-permute-start.5 = (bf16[128,1024]{1,0:T(8,128)(2,1)}, bf16[128,1024]{1,0:T(8,128)(2,1)S(1)}, u32[]{:S(2)}, u32[]{:S(2)}) collective-permute-start(bf16[128,1024]{1,0:T(8,128)(2,1)} %get-tuple-element.15), channel_id=1, source_target_pairs={{0,16},{8,24},{16,0},{24,8},{1,17},{9,25},{17,1},{25,9},{2,18},{10... | collective-permute-start | bytes 786440 | tf_op jit(solution)/shard_map/ppermute | solution.py:45
  14.3 13.6 %collective-permute-start.4 = (bf16[128,1024]{1,0:T(8,128)(2,1)}, bf16[128,1024]{1,0:T(8,128)(2,1)S(1)}, u32[]{:S(2)}, u32[]{:S(2)}) collective-permute-start(bf16[128,1024]{1,0:T(8,128)(2,1)} %get-tuple-element.16), channel_id=1, source_target_pairs={{0,8},{8,0},{16,24},{24,16},{1,9},{9,1},{17,25},{25,17},{2,10},{10... | collective-permute-start | bytes 786440 | tf_op jit(solution)/shard_map/ppermute | solution.py:45
  33.5 1.7 %collective-permute-start.7 = (f32[640,128]{1,0:T(8,128)S(1)}, f32[640,128]{1,0:T(8,128)S(1)}, u32[]{:S(2)}, u32[]{:S(2)}) collective-permute-start(f32[640,128]{1,0:T(8,128)S(1)} %dynamic-slice_bitcast_fusion), channel_id=1, source_target_pairs={{0,1},{1,0},{2,3},{3,2},{4,5},{5,4},{6,7},{7,6},{8,9},{9,8},{10,11... | collective-permute-start | bytes 983048 | tf_op jit(solution)/shard_map/ppermute | solution.py:45
  35.3 5.2 %collective-permute-start.8 = (f32[160,128]{1,0:T(8,128)S(1)}, f32[160,128]{1,0:T(8,128)S(1)}, u32[]{:S(2)}, u32[]{:S(2)}) collective-permute-start(f32[160,128]{1,0:T(8,128)S(1)} %get-tuple-element.27), channel_id=1, source_target_pairs={{0,8},{8,0},{16,24},{24,16},{1,9},{9,1},{17,25},{25,17},{2,10},{10... | collective-permute-start | bytes 245768 | tf_op jit(solution)/shard_map/ppermute | solution.py:45
  35.9 5.9 %collective-permute-start.10 = (f32[160,128]{1,0:T(8,128)S(1)}, f32[160,128]{1,0:T(8,128)S(1)}, u32[]{:S(2)}, u32[]{:S(2)}) collective-permute-start(f32[160,128]{1,0:T(8,128)S(1)} %get-tuple-element.28), channel_id=1, source_target_pairs={{0,24},{8,16},{16,8},{24,0},{1,25},{9,17},{17,9},{25,1},{2,26},{10... | collective-permute-start | bytes 245768 | tf_op jit(solution)/shard_map/ppermute | solution.py:45
  37.4 5.5 %collective-permute-start.9 = (f32[160,128]{1,0:T(8,128)S(1)}, f32[160,128]{1,0:T(8,128)S(1)}, u32[]{:S(2)}, u32[]{:S(2)}) collective-permute-start(f32[160,128]{1,0:T(8,128)S(1)} %get-tuple-element.29), channel_id=1, source_target_pairs={{0,16},{8,24},{16,0},{24,8},{1,17},{9,25},{17,1},{25,9},{2,18},{10... | collective-permute-start | bytes 245768 | tf_op jit(solution)/shard_map/ppermute | solution.py:45
  42.9 7.2 %collective-permute-start.13 = (f32[160,128]{1,0:T(8,128)S(1)}, f32[160,128]{1,0:T(8,128)S(1)}, u32[]{:S(2)}, u32[]{:S(2)}) collective-permute-start(f32[160,128]{1,0:T(8,128)S(1)} %fusion.1), channel_id=1, source_target_pairs={{0,6},{1,7},{2,4},{3,5},{4,2},{5,3},{6,0},{7,1},{8,14},{9,15},{10,... | collective-permute-start | bytes 245768 | tf_op jit(solution)/shard_map/ppermute | solution.py:45
  46.6 6.5 %collective-permute-start.12 = (f32[160,128]{1,0:T(8,128)S(1)}, f32[160,128]{1,0:T(8,128)S(1)}, u32[]{:S(2)}, u32[]{:S(2)}) collective-permute-start(f32[160,128]{1,0:T(8,128)S(1)} %fusion.1), channel_id=1, source_target_pairs={{0,4},{1,5},{2,6},{3,7},{4,0},{5,1},{6,2},{7,3},{8,12},{9,13},{10,... | collective-permute-start | bytes 245768 | tf_op jit(solution)/shard_map/ppermute | solution.py:45
  46.6 6.5 %collective-permute-start.11 = (f32[160,128]{1,0:T(8,128)S(1)}, f32[160,128]{1,0:T(8,128)S(1)}, u32[]{:S(2)}, u32[]{:S(2)}) collective-permute-start(f32[160,128]{1,0:T(8,128)S(1)} %fusion.1), channel_id=1, source_target_pairs={{0,2},{1,3},{2,0},{3,1},{4,6},{5,7},{6,4},{7,5},{8,10},{9,11},{10,... | collective-permute-start | bytes 245768 | tf_op jit(solution)/shard_map/ppermute | solution.py:45
  53.2 6.1 %collective-permute-start.16 = (f32[160,128]{1,0:T(8,128)S(1)}, f32[160,128]{1,0:T(8,128)S(1)}, u32[]{:S(2)}, u32[]{:S(2)}) collective-permute-start(f32[160,128]{1,0:T(8,128)S(1)} %add_add_fusion), channel_id=1, source_target_pairs={{0,24},{8,16},{16,8},{24,0},{1,25},{9,17},{17,9},{25,1},{2,26},{10... | collective-permute-start | bytes 245768 | tf_op jit(solution)/shard_map/ppermute | solution.py:45
  54.9 5.0 %collective-permute-start.15 = (f32[160,128]{1,0:T(8,128)S(1)}, f32[160,128]{1,0:T(8,128)S(1)}, u32[]{:S(2)}, u32[]{:S(2)}) collective-permute-start(f32[160,128]{1,0:T(8,128)S(1)} %add_add_fusion), channel_id=1, source_target_pairs={{0,16},{8,24},{16,0},{24,8},{1,17},{9,25},{17,1},{25,9},{2,18},{10... | collective-permute-start | bytes 245768 | tf_op jit(solution)/shard_map/ppermute | solution.py:45
  56.2 4.4 %collective-permute-start.14 = (f32[160,128]{1,0:T(8,128)S(1)}, f32[160,128]{1,0:T(8,128)S(1)}, u32[]{:S(2)}, u32[]{:S(2)}) collective-permute-start(f32[160,128]{1,0:T(8,128)S(1)} %add_add_fusion), channel_id=1, source_target_pairs={{0,8},{8,0},{16,24},{24,16},{1,9},{9,1},{17,25},{25,17},{2,10},{10... | collective-permute-start | bytes 245768 | tf_op jit(solution)/shard_map/ppermute | solution.py:45
  60.7 1.7 %collective-permute-start.17 = (f32[640,128]{1,0:T(8,128)S(1)}, f32[640,128]{1,0:T(8,128)S(1)}, u32[]{:S(2)}, u32[]{:S(2)}) collective-permute-start(f32[640,128]{1,0:T(8,128)S(1)} %pad_maximum_fusion.4), channel_id=1, source_target_pairs={{0,1},{1,0},{2,3},{3,2},{4,5},{5,4},{6,7},{7,6},{8,9},{9,8},{10,11... | collective-permute-start | bytes 983048 | tf_op jit(solution)/shard_map/ppermute | solution.py:45
where the time goes:
time: 70.4 us; the launch traced here: 70.2 us
  waiting for transfers between devices  31.1 us (44%)
  starting transfers between devices  19.8 us (28%)
  Pallas kernels  13.2 us (19%)
  local copies, waits for them, and re-layouts  4.87 us (7%)
  between operations  0.86 us (1%)
    ppermute x18, waiting for transfers between devices, swap(): return lax.ppermute(value, axis, [(i, i ^ mask) for i in range(size)])  31.1 us
    ppermute x18, starting transfers between devices, swap(): return lax.ppermute(value, axis, [(i, i ^ mask) for i in range(size)])  19.8 us
    pallas_call x1, Pallas kernels, finish(): pl.pallas_call(functools.partial(finish_kernel, tiles, scale), out_shape=...  7.68 us
    pallas_call x1, Pallas kernels, front(): pl.pallas_call(functools.partial(front_kernel, len(wanted), tiles, scale)...  5.55 us
    dynamic_slice x2, local copies, waits for them, and re-layouts, columns_of(): return lax.dynamic_slice_in_dim(array, index * width, width, axis=1)  3.31 us
  transfers between devices with their start and end apart: 18, of which 16 were waited for; matrix products, arithmetic and copies ran while one was open for 6% of the time, Pallas kernels for 0%

commit v1 on v0

v1 whole, which is shorter than its diff:
```python
import functools
import math

import jax
import jax.numpy as jnp
from jax import lax
from jax.experimental import pallas as pl
from jax.experimental.pallas import tpu as pltpu
from jax.sharding import PartitionSpec as P


LANES = 128

decay_rate = 0.95
linear_coef = 3.4445
square_coef = -4.775
quint_coef = 2.0315
epsilon = 1e-07
iterations = 2


ROWS_BY_ROWS = (((1,), (1,)), ((), ()))
COLUMNS_BY_ROWS = (((0,), (0,)), ((), ()))


def split(value):
    high = value.astype(jnp.bfloat16)
    low = (value - high.astype(jnp.float32)).astype(jnp.bfloat16)
    return high, low


def dot(left, right, dims=(((1,), (0,)), ((), ()))):
    return lax.dot_general(left, right, dims, preferred_element_type=jnp.float32)


def swap(value, axis, mask):
    size = lax.axis_size(axis)
    return lax.ppermute(value, axis, [(i, i ^ mask) for i in range(size)])


def pick(stack, index):
    return lax.dynamic_index_in_dim(stack, index, 0, keepdims=False)


def few(size):
    return size in (2, 4)


def scatter_sum(value, axis):
    size = lax.axis_size(axis)
    parts = value.reshape(size, value.shape[0] // size, *value.shape[1:])
    if not few(size):
        return jnp.sum(lax.all_to_all(parts, axis, 0, 0), axis=0)
    me = lax.axis_index(axis)
    arrived = [swap(pick(parts, me ^ mask), axis, mask) for mask in range(1, size)]
    total = pick(parts, me)
    for part in arrived:
        total = total + part
    return total


def gather(value, axis):
    size = lax.axis_size(axis)
    if not few(size):
        return lax.all_gather(value, axis, axis=0, tiled=True)
    me = lax.axis_index(axis)
    parts = jnp.stack([value] + [swap(value, axis, mask) for mask in range(1, size)])
    return jnp.concatenate([pick(parts, me ^ owner) for owner in range(size)], axis=0)


def sum_over_devices(packed):
    heads = lax.axis_size("head")
    core = lax.axis_index("head") % 2
    halves = packed.reshape(2, packed.shape[0] // 2, *packed.shape[1:])
    half = pick(halves, core) + swap(pick(halves, 1 - core), "head", 1)
    part = scatter_sum(half, "dp")
    if heads == 8:
        arrived = []
        for mask in range(1, 4):
            arrived.append(swap(part, "head", 2 * mask))
        part = (part + arrived[0]) + (arrived[1] + arrived[2])
    else:
        mask = 2
        while mask < heads:
            part = part + swap(part, "head", mask)
            mask *= 2
    half = gather(part, "dp")
    other = swap(half, "head", 1)
    return jnp.concatenate(
        [jnp.where(core == 0, half, other), jnp.where(core == 0, other, half)], axis=0
    )


def packed_rows(rows, pieces):
    blocks = rows // LANES
    folded = blocks // 2
    used = (blocks * (blocks - 1) // 2 + folded) * LANES + folded
    unit = 8 * pieces
    return -(-used // unit) * unit


def above(blocks):
    return [(i, j) for i in range(blocks) for j in range(i + 1, blocks)]


def block_at(index):
    return pl.ds(index * LANES, LANES)


def positions():
    row = lax.broadcasted_iota(jnp.int32, (LANES, LANES), 0)
    column = lax.broadcasted_iota(jnp.int32, (LANES, LANES), 1)
    return row, column


def pack(block_of, blocks, packed_ref):
    row, column = positions()
    slot = 0
    for i, j in above(blocks):
        packed_ref[block_at(slot), :] = block_of(i, j)
        slot += 1
    diagonals = []
    for i in range(0, blocks, 2):
        second = block_of(i + 1, i + 1)
        packed_ref[block_at(slot), :] = jnp.where(row <= column, block_of(i, i), second)
        diagonals.append(jnp.sum(jnp.where(row == column, second, 0.0), axis=0, keepdims=True))
        slot += 1
    start = slot * LANES
    rest = packed_ref.shape[0] - start
    place = lax.broadcasted_iota(jnp.int32, (rest, LANES), 0)
    tail = jnp.zeros((rest, LANES), jnp.float32)
    for k, diagonal in enumerate(diagonals):
        tail = jnp.where(place == k, diagonal, tail)
    packed_ref[pl.ds(start, rest), :] = tail


def unpack(packed_ref, blocks, square_ref):
    row, column = positions()
    slot = 0
    for i, j in above(blocks):
        block = packed_ref[block_at(slot), :]
        square_ref[block_at(i), block_at(j)] = block
        square_ref[block_at(j), block_at(i)] = block.T
        slot += 1
    start = (slot + blocks // 2) * LANES
    trace = jnp.zeros((1, 1), jnp.float32)
    for i in range(0, blocks, 2):
        block = packed_ref[block_at(slot), :]
        turned = block.T
        diagonal = packed_ref[pl.ds(start + i // 2, 1), :]
        square_ref[block_at(i), block_at(i)] = jnp.where(row <= column, block, turned)
        square_ref[block_at(i + 1), block_at(i + 1)] = jnp.where(
            row > column, block, jnp.where(row < column, turned, diagonal)
        )
        trace = trace + jnp.sum(jnp.where(row == column, block, 0.0), keepdims=True)
        trace = trace + jnp.sum(diagonal, keepdims=True)
        slot += 1
    return trace


def tile_rows(i, j, tiles):
    return pl.ds(i * 8 * tiles + j, 8, stride=tiles)


def momentum_rows(ref, start, j, tiles):
    return jnp.concatenate(
        [ref[pl.ds((start + part) * tiles + j, 8, stride=tiles), :] for part in (0, 8)], axis=0
    )


def front_kernel(arrivals, tiles, scale, *refs):
    (lat_ref, weight_ref), refs = refs[:2], refs[2:]
    wanted_refs, refs = refs[:arrivals], refs[arrivals:]
    (targets_ref, momentum_ref, gradient_ref, packed_ref), refs = refs[:4], refs[4:]
    mine, old, residual, high_ref, low_ref, sems = refs
    rows, width = high_ref.shape
    load = pltpu.make_async_copy(momentum_ref, old, sems.at[0])
    arrived = sum(wanted_ref.shape[0] for wanted_ref in wanted_refs)
    if arrived < lat_ref.shape[0]:
        first = pl.multiple_of(lax.axis_index("dp") * width, width)
        own = pltpu.make_async_copy(targets_ref.at[:, pl.ds(first, width)], mine, sems.at[1])
        own.start()
        wanted_refs = (*wanted_refs, mine)
    load.start()
    start = 0
    for wanted_ref in wanted_refs:
        count = wanted_ref.shape[0]
        here = pl.ds(start, count)
        predicted = dot(lat_ref[here, :], weight_ref[...])
        if start == arrived:
            own.wait()
        residual[here, :] = (predicted - wanted_ref[...].astype(jnp.float32)).astype(jnp.bfloat16)
        start += count
    load.wait()
    for block in range(rows // LANES):
        first = block * LANES
        gradient = dot(lat_ref[:, block_at(block)], residual[...], COLUMNS_BY_ROWS) * scale
        gradient_ref[block_at(block), :] = gradient
        for i in range(0, LANES, 16):
            for j in range(tiles):
                piece = gradient[i : i + 16, j * LANES : (j + 1) * LANES]
                fresh = decay_rate * momentum_rows(old, first + i, j, tiles) + piece
                high, low = split(piece + decay_rate * fresh)
                here = (pl.ds(first + i, 16), block_at(j))
                high_ref[here] = high
                low_ref[here] = low
    half = rows // 2

    def gram(i, j):
        left, right = pl.ds(i * half, half), pl.ds(j * half, half)
        return (
            dot(high_ref[left, :], low_ref[right, :], ROWS_BY_ROWS)
            + dot(low_ref[left, :], high_ref[right, :], ROWS_BY_ROWS)
            + dot(high_ref[left, :], high_ref[right, :], ROWS_BY_ROWS)
        )

    quarters = {(0, 0): gram(0, 0), (0, 1): gram(0, 1), (1, 1): gram(1, 1)}
    per = half // LANES

    def block_of(i, j):
        quarter = quarters[i // per, j // per]
        i, j = i % per, j % per
        return quarter[i * LANES : (i + 1) * LANES, j * LANES : (j + 1) * LANES]

    pack(block_of, rows // LANES, packed_ref)


def in_hbm(array):
    return pltpu.with_memory_space_constraint(array, pltpu.HBM)


def front(lat, weight, wanted, targets, momentum, scale, pieces):
    rows, width = weight.shape
    vmem = pl.BlockSpec(memory_space=pltpu.VMEM)
    hbm = pl.BlockSpec(memory_space=pl.ANY)
    return pl.pallas_call(
        functools.partial(front_kernel, len(wanted), width // LANES, scale),
        out_shape=(
            pltpu.VMEM((rows, width), jnp.float32),
            pltpu.VMEM((packed_rows(rows, pieces), LANES), jnp.float32),
        ),
        in_specs=[vmem] * (2 + len(wanted)) + [hbm, hbm],
        out_specs=(vmem, vmem),
        scratch_shapes=[
            pltpu.VMEM((targets.shape[0], width), targets.dtype),
            pltpu.VMEM(momentum.shape, jnp.float32),
            pltpu.VMEM((lat.shape[0], width), jnp.bfloat16),
            pltpu.VMEM((rows, width), jnp.bfloat16),
            pltpu.VMEM((rows, width), jnp.bfloat16),
            pltpu.SemaphoreType.DMA((2,)),
        ],
        compiler_params=pltpu.CompilerParams(vmem_limit_bytes=24 << 20),
        name="front",
    )(lat, weight, *wanted, in_hbm(targets), in_hbm(momentum))


def momentum_kernel(tiles, gradient_ref, old, new, high_ref, low_ref):
    for i in range(0, gradient_ref.shape[0], 16):
        for j in range(tiles):
            here = (pl.ds(i, 16), block_at(j))
            piece = gradient_ref[here]
            fresh = decay_rate * momentum_rows(old, i, j, tiles) + piece
            for part in (0, 8):
                new[tile_rows((i + part) // 8, j, tiles), :] = fresh[part : part + 8]
            high_ref[here], low_ref[here] = split(piece + decay_rate * fresh)


def momentum_step(gradient, momentum):
    rows, width = gradient.shape
    tiles = width // LANES
    half = pltpu.HBM((rows, width), jnp.bfloat16)
    wide = pl.BlockSpec((LANES, width), lambda i: (i, 0))
    linear = pl.BlockSpec((LANES * tiles, LANES), lambda i: (i, 0))
    return pl.pallas_call(
        functools.partial(momentum_kernel, tiles),
        out_shape=(pltpu.HBM(momentum.shape, jnp.float32), half, half),
        grid=(rows // LANES,),
        in_specs=[wide, linear],
        out_specs=(linear, wide, wide),
        compiler_params=pltpu.CompilerParams(vmem_limit_bytes=16 << 20),
        name="momentum_step",
    )(gradient, in_hbm(momentum))


def symmetric_product(left, right):
    (left_high, left_low), (right_high, right_low) = left, right
    half = left_high.shape[0] // 2

    def part(i, j):
        rows, columns = slice(i * half, (i + 1) * half), slice(j * half, (j + 1) * half)
        return (
            dot(left_high[rows], right_low[:, columns])
            + dot(left_low[rows], right_high[:, columns])
            + dot(left_high[rows], right_high[:, columns])
        )

    corner, side, last = part(0, 0), part(0, 1), part(1, 1)
    return jnp.concatenate(
        [jnp.concatenate([corner, side], axis=1), jnp.concatenate([side.T, last], axis=1)], axis=0
    )


def finish_kernel(
    tiles, scale, packed_ref, high_hbm, low_hbm, out_hbm, square_ref, high_ref, low_ref, out, sems
):
    loads = [
        pltpu.make_async_copy(high_hbm, high_ref, sems.at[0]),
        pltpu.make_async_copy(low_hbm, low_ref, sems.at[1]),
    ]
    for load in loads:
        load.start()
    rows = square_ref.shape[0]
    squares = unpack(packed_ref, rows // LANES, square_ref)
    inverse = 1.0 / (jnp.sqrt(squares) + epsilon)
    gram = (square_ref[...] * inverse) * inverse
    row = lax.broadcasted_iota(jnp.int32, gram.shape, 0)
    column = lax.broadcasted_iota(jnp.int32, gram.shape, 1)
    identity = jnp.where(row == column, linear_coef, 0.0)
    total = None
    for iteration in range(iterations):
        parts = split(gram)
        factor = (
            identity + square_coef * gram + quint_coef * symmetric_product(parts, parts)
        )
        factor_parts = split(factor)
        total = factor if total is None else symmetric_product(split(total), factor_parts)
        if iteration + 1 < iterations:
            once = symmetric_product(parts, factor_parts)
            gram = symmetric_product(split(once), factor_parts)
    left_high, left_low = split(total * (inverse * scale))
    for load in loads:
        load.wait()
    stores = []
    for block in range(rows // LANES):
        here = slice(block * LANES, (block + 1) * LANES)
        result = (
            dot(left_high[here], low_ref[...])
            + dot(left_low[here], high_ref[...])
            + dot(left_high[here], high_ref[...])
        )
        for i in range(LANES // 8):
            for j in range(tiles):
                out[tile_rows(block * LANES // 8 + i, j, tiles), :] = result[
                    i * 8 : (i + 1) * 8, j * LANES : (j + 1) * LANES
                ]
        chunk = pl.ds(block * LANES * tiles, LANES * tiles)
        store = pltpu.make_async_copy(out.at[chunk, :], out_hbm.at[chunk, :], sems.at[2 + block])
        store.start()
        stores.append(store)
    for store in stores:
        store.wait()


def finish(packed, high, low, scale):
    rows, width = high.shape
    tiles = width // LANES
    linear = (rows * tiles, LANES)
    vmem = pl.BlockSpec(memory_space=pltpu.VMEM)
    hbm = pl.BlockSpec(memory_space=pl.ANY)
    return pl.pallas_call(
        functools.partial(finish_kernel, tiles, scale),
        out_shape=pltpu.HBM(linear, jnp.float32),
        in_specs=[vmem, hbm, hbm],
        out_specs=hbm,
        scratch_shapes=[
            pltpu.VMEM((rows, rows), jnp.float32),
            pltpu.VMEM((rows, width), jnp.bfloat16),
            pltpu.VMEM((rows, width), jnp.bfloat16),
            pltpu.VMEM(linear, jnp.float32),
            pltpu.SemaphoreType.DMA((2 + rows // LANES,)),
        ],
        compiler_params=pltpu.CompilerParams(vmem_limit_bytes=28 << 20),
        name="finish",
    )(packed, in_hbm(high), in_hbm(low))


def columns_of(array, index, width):
    return lax.dynamic_slice_in_dim(array, index * width, width, axis=1)


def gather_tokens(latents, targets, width):
    groups = lax.axis_size("dp")
    if not few(groups):
        lat = lax.all_gather(latents, "dp", axis=0, tiled=True)
        wanted = lax.all_to_all(targets, "dp", split_axis=1, concat_axis=0, tiled=True)
        return lat, [wanted]
    me = lax.axis_index("dp")
    core = lax.axis_index("head") % 2
    tokens, rows = latents.shape
    mine = pick(latents.reshape(2, tokens // 2, rows), core)
    wanted = [columns_of(targets, me ^ mask, width) for mask in range(1, groups)]
    first = []
    for mask in range(1, groups):
        first.append(swap(mine, "dp", mask))
    first = jnp.stack(first)
    second = swap(first, "head", 1)
    others = jnp.stack(
        [jnp.where(core == 0, first, second), jnp.where(core == 0, second, first)], axis=1
    )
    lat = jnp.concatenate([others.reshape((groups - 1) * tokens, rows), latents], axis=0)
    arrived = []
    for mask in range(1, groups):
        arrived.append(swap(wanted[mask - 1], "dp", mask))
    return lat, arrived


def local(total_columns, latents, targets, kv_weight, momentum):
    rows = momentum.shape[0]
    width = momentum.shape[2]
    weight = columns_of(kv_weight, lax.axis_index("dp"), width)
    lat, wanted = gather_tokens(latents, targets, width)
    momentum = momentum.reshape(rows * width // LANES, LANES)
    scale = 1.0 / math.sqrt(lat.shape[0])
    gradient, packed = front(lat, weight, wanted, targets, momentum, scale, 2 * lax.axis_size("dp"))
    momentum_new, high, low = momentum_step(gradient, momentum)
    packed = sum_over_devices(packed)
    update = finish(packed, high, low, math.sqrt(total_columns))
    return momentum_new.reshape(rows, 1, width), update.reshape(rows, 1, width)


def solution(mesh):

    def step(latents, targets, kv_weight, momentum):
        total_columns = kv_weight.shape[1]
        return jax.shard_map(
            functools.partial(local, total_columns),
            mesh=mesh,
            in_specs=(P("dp", None), P("dp", "head"), P(None, "head"), P(None, "head", "dp")),
            out_specs=(P(None, "head", "dp"), P(None, "head", "dp")),
            check_vma=False,
        )(latents, targets, kv_weight, momentum)

    return step
```

time: 70.4 us -> 69.6 us (0.989)
  Pallas kernels: 13.2 us -> 16.4 us
  waiting for transfers between devices: 31.1 us -> 28.4 us
  local copies, waits for them, and re-layouts: 4.87 us -> 3.41 us
    pallas_call x1 -> x2, Pallas kernels: 5.55 us -> 9.53 us  [the longest x1 5 us: front(): pl.pallas_call(functools.partial(front_kernel, len(wanted), width // LANE...]
    ppermute x18, waiting for transfers between devices: 31.1 us -> 28.4 us  [swap(): return lax.ppermute(value, axis, [(i, i ^ mask) for i in range(size)])]
    dynamic_slice x2, local copies, waits for them, and re-layouts: 3.31 us -> 2.46 us  [columns_of(): return lax.dynamic_slice_in_dim(array, index * width, width, axis=1)]
    pallas_call x1, Pallas kernels: 7.68 us -> 6.89 us  [finish(): pl.pallas_call(functools.partial(finish_kernel, tiles, scale), out_shape=...]
  transfers between devices with their start and end apart: 18 -> 18, of which waited for: 16 -> 15; matrix products, arithmetic and copies ran while one was open for 6% -> 4% of each run, Pallas kernels for 0% -> 7%
where the time goes in v1:
time: 69.6 us; the launch traced here: 69.3 us
  waiting for transfers between devices  28.4 us (41%)
  starting transfers between devices  19.8 us (28%)
  Pallas kernels  16.4 us (24%)
  local copies, waits for them, and re-layouts  3.41 us (5%)
  between operations  0.83 us (1%)
    ppermute x18, waiting for transfers between devices, swap(): return lax.ppermute(value, axis, [(i, i ^ mask) for i in range(size)])  28.4 us
    ppermute x18, starting transfers between devices, swap(): return lax.ppermute(value, axis, [(i, i ^ mask) for i in range(size)])  19.8 us
    pallas_call x1, Pallas kernels, finish(): pl.pallas_call(functools.partial(finish_kernel, tiles, scale), out_shape=...  6.89 us
    pallas_call x1, Pallas kernels, front(): pl.pallas_call(functools.partial(front_kernel, len(wanted), width // LANE...  5 us
    pallas_call x1, Pallas kernels, momentum_step(): pl.pallas_call(functools.partial(momentum_kernel, tiles), out_shape=(pltp...  4.53 us
    dynamic_slice x2, local copies, waits for them, and re-layouts, columns_of(): return lax.dynamic_slice_in_dim(array, index * width, width, axis=1)  2.46 us
  transfers between devices with their start and end apart: 18, of which 15 were waited for; matrix products, arithmetic and copies ran while one was open for 4% of the time, Pallas kernels for 7%

profile of v1, /device:TPU:0, one launch (start us, length us, event | category | flops | bytes accessed | tf_op | source)
XLA Modules:
  0.0 69.3 jit_solution(7262132002078036015)
XLA Ops:
  0.6 0.8 %dynamic-slice_bitcast_fusion.8 = bf16[64,512]{1,0:T(8,128)(2,1)S(1)} fusion(bf16[2,64,512]{2,1,0:T(8,128)(2,1)} %bitcast.54, s32[]{:T(128)S(6)} %select_n.73), kind=kLoop, calls=%fused_computation.23 | loop fusion | bytes 131076 | tf_op jit(solution)/shard_map/jit(dynamic_index_in_dim)/squeeze | solution.py:42
  1.5 3.9 %collective-permute-start.2 = (bf16[64,512]{1,0:T(8,128)(2,1)S(1)}, bf16[64,512]{1,0:T(8,128)(2,1)S(1)}, u32[]{:S(2)}, u32[]{:S(2)}) collective-permute-start(bf16[64,512]{1,0:T(8,128)(2,1)S(1)} %dynamic-slice_bitcast_fusion.8), channel_id=1, source_target_pairs={{0,24},{8,16},{16,8},{24,0},{1,25},{9,17},{17,9},{25,1},{2,26},{10... | collective-permute-start | bytes 196616 | tf_op jit(solution)/shard_map/ppermute | solution.py:38
  5.4 0.5 collective-permute-start.1
  5.9 0.1 collective-permute-start
  6.0 1.7 %collective-permute-done.2 = bf16[64,512]{1,0:T(8,128)(2,1)S(1)} collective-permute-done((bf16[64,512]{1,0:T(8,128)(2,1)S(1)}, bf16[64,512]{1,0:T(8,128)(2,1)S(1)}, u32[]{:S(2)}, u32[]{:S(2)}) %collective-permute-start.2) | collective-permute-done | bytes 65568 | tf_op jit(solution)/shard_map/ppermute | solution.py:38
  7.7 2.0 %collective-permute-done.1 = bf16[64,512]{1,0:T(8,128)(2,1)S(1)} collective-permute-done((bf16[64,512]{1,0:T(8,128)(2,1)S(1)}, bf16[64,512]{1,0:T(8,128)(2,1)S(1)}, u32[]{:S(2)}, u32[]{:S(2)}) %collective-permute-start.1) | collective-permute-done | bytes 65568 | tf_op jit(solution)/shard_map/ppermute | solution.py:38
  9.7 0.5 collective-permute-done
  10.2 0.1 collective-permute-start.3
  10.3 1.2 %constant_dynamic-slice_fusion = (bf16[128,1024]{1,0:T(8,128)(2,1)S(1)}, bf16[128,1024]{1,0:T(8,128)(2,1)S(1)}, bf16[128,1024]{1,0:T(8,128)(2,1)S(1)}) fusion(bf16[128,4096]{1,0:T(8,128)(2,1)} %refs_5_.1, s32[]{:T(128)S(6)} %select_n.79, s32[]{:T(128)S(6)} %select_n.78, s32[]{:T(128)S(6)} %select_n.77), kind=kLoop, calls=%fused_computation.24 | loop fusion | bytes 1572876 | tf_op jit(solution)/shard_map/dynamic_slice | solution.py:378
  11.5 0.0 copy-start
  11.5 1.6 %collective-permute-start.6 = (bf16[128,1024]{1,0:T(8,128)(2,1)S(1)}, bf16[128,1024]{1,0:T(8,128)(2,1)S(1)}, u32[]{:S(2)}, u32[]{:S(2)}) collective-permute-start(bf16[128,1024]{1,0:T(8,128)(2,1)S(1)} %get-tuple-element.14), channel_id=1, source_target_pairs={{0,24},{8,16},{16,8},{24,0},{1,25},{9,17},{17,9},{25,1},{2,26},{10... | collective-permute-start | bytes 786440 | tf_op jit(solution)/shard_map/ppermute | solution.py:38
  13.0 0.4 collective-permute-start.5
  13.5 1.6 %collective-permute-start.4 = (bf16[128,1024]{1,0:T(8,128)(2,1)S(1)}, bf16[128,1024]{1,0:T(8,128)(2,1)S(1)}, u32[]{:S(2)}, u32[]{:S(2)}) collective-permute-start(bf16[128,1024]{1,0:T(8,128)(2,1)S(1)} %get-tuple-element.16), channel_id=1, source_target_pairs={{0,8},{8,0},{16,24},{24,16},{1,9},{9,1},{17,25},{25,17},{2,10},{10... | collective-permute-start | bytes 786440 | tf_op jit(solution)/shard_map/ppermute | solution.py:38
  15.0 1.3 %constant_dynamic-slice_fusion.3.refs_1_ = bf16[512,1024]{1,0:T(8,128)(2,1)S(1)} fusion(bf16[512,4096]{1,0:T(8,128)(2,1)} %param.6, s32[]{:T(128)S(6)} %select_n.76), kind=kLoop, calls=%fused_computation.27 | loop fusion | bytes 2097156 | tf_op jit(solution)/shard_map/dynamic_slice | solution.py:378
  16.3 0.0 collective-permute-done.3
  16.4 0.0 copy-done
  16.5 5.2 %collective-permute-done.6.refs_4_ = bf16[128,1024]{1,0:T(8,128)(2,1)S(1)} collective-permute-done((bf16[128,1024]{1,0:T(8,128)(2,1)S(1)}, bf16[128,1024]{1,0:T(8,128)(2,1)S(1)}, u32[]{:S(2)}, u32[]{:S(2)}) %collective-permute-start.6) | collective-permute-done | bytes 262176 | tf_op jit(solution)/shard_map/ppermute | solution.py:38
  21.7 5.1 %collective-permute-done.5.refs_3_ = bf16[128,1024]{1,0:T(8,128)(2,1)S(1)} collective-permute-done((bf16[128,1024]{1,0:T(8,128)(2,1)S(1)}, bf16[128,1024]{1,0:T(8,128)(2,1)S(1)}, u32[]{:S(2)}, u32[]{:S(2)}) %collective-permute-start.5) | collective-permute-done | bytes 262176 | tf_op jit(solution)/shard_map/ppermute | solution.py:38
  26.8 0.1 collective-permute-done.4.refs_2_
  26.9 5.0 %front.1 = (f32[512,1024]{1,0:T(8,128)S(1)}, f32[1088,128]{1,0:T(8,128)S(1)}) custom-call(bf16[512,512]{1,0:T(8,128)(2,1)S(1)} %pad_maximum_fusion.1.refs_0_, bf16[512,1024]{1,0:T(8,128)(2,1)S(1)} %constant_dynamic-slice_fusion.3.refs_1_, bf16[128,1024]{1,0:T(8,128)(2,1)S(1)} %collective-permute-done.4.refs_2_, ...), custom_call_target="tpu_custom_call" | custom-call | tf_op jit(solution)/shard_map/front/pallas_call | solution.py:236
  31.9 0.1 collective-permute-start.7
  32.0 1.5 %collective-permute-done.7 = f32[544,128]{1,0:T(8,128)S(1)} collective-permute-done((f32[544,128]{1,0:T(8,128)S(1)}, f32[544,128]{1,0:T(8,128)S(1)}, u32[]{:S(2)}, u32[]{:S(2)}) %collective-permute-start.7) | collective-permute-done | bytes 278560 | tf_op jit(solution)/shard_map/ppermute | solution.py:38
  33.6 0.6 collective-permute-start.8
  34.2 1.6 %collective-permute-start.10 = (f32[136,128]{1,0:T(8,128)S(1)}, f32[136,128]{1,0:T(8,128)S(1)}, u32[]{:S(2)}, u32[]{:S(2)}) collective-permute-start(f32[136,128]{1,0:T(8,128)S(1)} %get-tuple-element.26), channel_id=1, source_target_pairs={{0,24},{8,16},{16,8},{24,0},{1,25},{9,17},{17,9},{25,1},{2,26},{10... | collective-permute-start | bytes 208904 | tf_op jit(solution)/shard_map/ppermute | solution.py:38
  35.8 1.4 %collective-permute-start.9 = (f32[136,128]{1,0:T(8,128)S(1)}, f32[136,128]{1,0:T(8,128)S(1)}, u32[]{:S(2)}, u32[]{:S(2)}) collective-permute-start(f32[136,128]{1,0:T(8,128)S(1)} %get-tuple-element.27), channel_id=1, source_target_pairs={{0,16},{8,24},{16,0},{24,8},{1,17},{9,25},{17,1},{25,9},{2,18},{10... | collective-permute-start | bytes 208904 | tf_op jit(solution)/shard_map/ppermute | solution.py:38
  37.2 1.3 %collective-permute-done.8 = f32[136,128]{1,0:T(8,128)S(1)} collective-permute-done((f32[136,128]{1,0:T(8,128)S(1)}, f32[136,128]{1,0:T(8,128)S(1)}, u32[]{:S(2)}, u32[]{:S(2)}) %collective-permute-start.8) | collective-permute-done | bytes 69664 | tf_op jit(solution)/shard_map/ppermute | solution.py:38
  38.4 1.2 %collective-permute-done.10 = f32[136,128]{1,0:T(8,128)S(1)} collective-permute-done((f32[136,128]{1,0:T(8,128)S(1)}, f32[136,128]{1,0:T(8,128)S(1)}, u32[]{:S(2)}, u32[]{:S(2)}) %collective-permute-start.10) | collective-permute-done | bytes 69664 | tf_op jit(solution)/shard_map/ppermute | solution.py:38
  39.6 1.1 %collective-permute-done.9 = f32[136,128]{1,0:T(8,128)S(1)} collective-permute-done((f32[136,128]{1,0:T(8,128)S(1)}, f32[136,128]{1,0:T(8,128)S(1)}, u32[]{:S(2)}, u32[]{:S(2)}) %collective-permute-start.9) | collective-permute-done | bytes 69664 | tf_op jit(solution)/shard_map/ppermute | solution.py:38
  40.8 3.7 %collective-permute-start.13 = (f32[136,128]{1,0:T(8,128)S(1)}, f32[136,128]{1,0:T(8,128)S(1)}, u32[]{:S(2)}, u32[]{:S(2)}) collective-permute-start(f32[136,128]{1,0:T(8,128)S(1)} %fusion.1), channel_id=1, source_target_pairs={{0,6},{1,7},{2,4},{3,5},{4,2},{5,3},{6,0},{7,1},{8,14},{9,15},{10,... | collective-permute-start | bytes 208904 | tf_op jit(solution)/shard_map/ppermute | solution.py:38
  44.5 0.0 collective-permute-start.12
  44.5 0.7 %collective-permute-start.11 = (f32[136,128]{1,0:T(8,128)S(1)}, f32[136,128]{1,0:T(8,128)S(1)}, u32[]{:S(2)}, u32[]{:S(2)}) collective-permute-start(f32[136,128]{1,0:T(8,128)S(1)} %fusion.1), channel_id=1, source_target_pairs={{0,2},{1,3},{2,0},{3,1},{4,6},{5,7},{6,4},{7,5},{8,10},{9,11},{10,... | collective-permute-start | bytes 208904 | tf_op jit(solution)/shard_map/ppermute | solution.py:38
  45.2 2.3 %collective-permute-done.13 = f32[136,128]{1,0:T(8,128)S(1)} collective-permute-done((f32[136,128]{1,0:T(8,128)S(1)}, f32[136,128]{1,0:T(8,128)S(1)}, u32[]{:S(2)}, u32[]{:S(2)}) %collective-permute-start.13) | collective-permute-done | bytes 69664 | tf_op jit(solution)/shard_map/ppermute | solution.py:38
  47.5 2.7 %collective-permute-done.12 = f32[136,128]{1,0:T(8,128)S(1)} collective-permute-done((f32[136,128]{1,0:T(8,128)S(1)}, f32[136,128]{1,0:T(8,128)S(1)}, u32[]{:S(2)}, u32[]{:S(2)}) %collective-permute-start.12) | collective-permute-done | bytes 69664 | tf_op jit(solution)/shard_map/ppermute | solution.py:38
  50.2 0.0 collective-permute-done.11
  50.2 1.7 %collective-permute-start.16 = (f32[136,128]{1,0:T(8,128)S(1)}, f32[136,128]{1,0:T(8,128)S(1)}, u32[]{:S(2)}, u32[]{:S(2)}) collective-permute-start(f32[136,128]{1,0:T(8,128)S(1)} %add_add_fusion), channel_id=1, source_target_pairs={{0,24},{8,16},{16,8},{24,0},{1,25},{9,17},{17,9},{25,1},{2,26},{10... | collective-permute-start | bytes 208904 | tf_op jit(solution)/shard_map/ppermute | solution.py:38
  51.9 1.4 %collective-permute-start.15 = (f32[136,128]{1,0:T(8,128)S(1)}, f32[136,128]{1,0:T(8,128)S(1)}, u32[]{:S(2)}, u32[]{:S(2)}) collective-permute-start(f32[136,128]{1,0:T(8,128)S(1)} %add_add_fusion), channel_id=1, source_target_pairs={{0,16},{8,24},{16,0},{24,8},{1,17},{9,25},{17,1},{25,9},{2,18},{10... | collective-permute-start | bytes 208904 | tf_op jit(solution)/shard_map/ppermute | solution.py:38
  53.2 0.5 collective-permute-start.14
  53.8 2.2 %collective-permute-done.16 = f32[136,128]{1,0:T(8,128)S(1)} collective-permute-done((f32[136,128]{1,0:T(8,128)S(1)}, f32[136,128]{1,0:T(8,128)S(1)}, u32[]{:S(2)}, u32[]{:S(2)}) %collective-permute-start.16) | collective-permute-done | bytes 69664 | tf_op jit(solution)/shard_map/ppermute | solution.py:38
  56.0 0.6 collective-permute-done.15
  56.6 1.0 %collective-permute-done.14 = f32[136,128]{1,0:T(8,128)S(1)} collective-permute-done((f32[136,128]{1,0:T(8,128)S(1)}, f32[136,128]{1,0:T(8,128)S(1)}, u32[]{:S(2)}, u32[]{:S(2)}) %collective-permute-start.14) | collective-permute-done | bytes 69664 | tf_op jit(solution)/shard_map/ppermute | solution.py:38
  57.7 0.1 collective-permute-start.17
  57.7 4.5 %momentum_step.1 = (f32[4096,128]{1,0:T(8,128)}, bf16[512,1024]{1,0:T(8,128)(2,1)}, bf16[512,1024]{1,0:T(8,128)(2,1)}) custom-call(f32[512,1024]{1,0:T(8,128)S(1)} %get-tuple-element.7.gradient_ref, f32[4096,128]{1,0:T(8,128)} %bitcast.49), custom_call_target="tpu_custom_call" | custom-call | tf_op jit(solution)/shard_map/momentum_step/pallas_call | solution.py:274
  62.3 0.0 collective-permute-done.17
  62.4 6.9 %finish.1 = f32[4096,128]{1,0:T(8,128)} custom-call(f32[1088,128]{1,0:T(8,128)S(1)} %pad_maximum_fusion.packed_ref, bf16[512,1024]{1,0:T(8,128)(2,1)} %get-tuple-element.10.high_hbm, bf16[512,1024]{1,0:T(8,128)(2,1)} %get-tuple-element.11.low_hbm), custom_call_target="tpu_custom_call" | custom-call | tf_op jit(solution)/shard_map/finish/pallas_call | solution.py:360
  (14 shorter events, 0.4 us)
Async XLA Ops:
  1.5 6.2 %collective-permute-start.2 = (bf16[64,512]{1,0:T(8,128)(2,1)S(1)}, bf16[64,512]{1,0:T(8,128)(2,1)S(1)}, u32[]{:S(2)}, u32[]{:S(2)}) collective-permute-start(bf16[64,512]{1,0:T(8,128)(2,1)S(1)} %dynamic-slice_bitcast_fusion.8), channel_id=1, source_target_pairs={{0,24},{8,16},{16,8},{24,0},{1,25},{9,17},{17,9},{25,1},{2,26},{10... | collective-permute-start | bytes 196616 | tf_op jit(solution)/shard_map/ppermute | solution.py:38
  5.4 4.3 %collective-permute-start.1 = (bf16[64,512]{1,0:T(8,128)(2,1)S(1)}, bf16[64,512]{1,0:T(8,128)(2,1)S(1)}, u32[]{:S(2)}, u32[]{:S(2)}) collective-permute-start(bf16[64,512]{1,0:T(8,128)(2,1)S(1)} %dynamic-slice_bitcast_fusion.8), channel_id=1, source_target_pairs={{0,16},{8,24},{16,0},{24,8},{1,17},{9,25},{17,1},{25,9},{2,18},{10... | collective-permute-start | bytes 196616 | tf_op jit(solution)/shard_map/ppermute | solution.py:38
  5.9 4.3 %collective-permute-start = (bf16[64,512]{1,0:T(8,128)(2,1)S(1)}, bf16[64,512]{1,0:T(8,128)(2,1)S(1)}, u32[]{:S(2)}, u32[]{:S(2)}) collective-permute-start(bf16[64,512]{1,0:T(8,128)(2,1)S(1)} %dynamic-slice_bitcast_fusion.8), channel_id=1, source_target_pairs={{0,8},{8,0},{16,24},{24,16},{1,9},{9,1},{17,25},{25,17},{2,10},{10... | collective-permute-start | bytes 196616 | tf_op jit(solution)/shard_map/ppermute | solution.py:38
  10.2 6.1 %collective-permute-start.3 = (bf16[3,64,512]{2,1,0:T(8,128)(2,1)S(1)}, bf16[3,64,512]{2,1,0:T(8,128)(2,1)S(1)}, u32[]{:S(2)}, u32[]{:S(2)}) collective-permute-start(bf16[3,64,512]{2,1,0:T(8,128)(2,1)S(1)} %pad_maximum_fusion.5), channel_id=1, source_target_pairs={{0,1},{1,0},{2,3},{3,2},{4,5},{5,4},{6,7},{7,6},{8,9},{9,8},{10,11... | collective-permute-start | bytes 589832 | tf_op jit(solution)/shard_map/ppermute | solution.py:38
  11.5 5.0 %copy-start = (bf16[128,512]{1,0:T(8,128)(2,1)S(1)}, bf16[128,512]{1,0:T(8,128)(2,1)}, u32[]{:S(2)}) copy-start(bf16[128,512]{1,0:T(8,128)(2,1)} %param.4) | copy-start | bytes 393220
  11.5 10.2 %collective-permute-start.6 = (bf16[128,1024]{1,0:T(8,128)(2,1)S(1)}, bf16[128,1024]{1,0:T(8,128)(2,1)S(1)}, u32[]{:S(2)}, u32[]{:S(2)}) collective-permute-start(bf16[128,1024]{1,0:T(8,128)(2,1)S(1)} %get-tuple-element.14), channel_id=1, source_target_pairs={{0,24},{8,16},{16,8},{24,0},{1,25},{9,17},{17,9},{25,1},{2,26},{10... | collective-permute-start | bytes 786440 | tf_op jit(solution)/shard_map/ppermute | solution.py:38
  13.0 13.7 %collective-permute-start.5 = (bf16[128,1024]{1,0:T(8,128)(2,1)S(1)}, bf16[128,1024]{1,0:T(8,128)(2,1)S(1)}, u32[]{:S(2)}, u32[]{:S(2)}) collective-permute-start(bf16[128,1024]{1,0:T(8,128)(2,1)S(1)} %get-tuple-element.15), channel_id=1, source_target_pairs={{0,16},{8,24},{16,0},{24,8},{1,17},{9,25},{17,1},{25,9},{2,18},{10... | collective-permute-start | bytes 786440 | tf_op jit(solution)/shard_map/ppermute | solution.py:38
  13.5 13.4 %collective-permute-start.4 = (bf16[128,1024]{1,0:T(8,128)(2,1)S(1)}, bf16[128,1024]{1,0:T(8,128)(2,1)S(1)}, u32[]{:S(2)}, u32[]{:S(2)}) collective-permute-start(bf16[128,1024]{1,0:T(8,128)(2,1)S(1)} %get-tuple-element.16), channel_id=1, source_target_pairs={{0,8},{8,0},{16,24},{24,16},{1,9},{9,1},{17,25},{25,17},{2,10},{10... | collective-permute-start | bytes 786440 | tf_op jit(solution)/shard_map/ppermute | solution.py:38
  31.9 1.6 %collective-permute-start.7 = (f32[544,128]{1,0:T(8,128)S(1)}, f32[544,128]{1,0:T(8,128)S(1)}, u32[]{:S(2)}, u32[]{:S(2)}) collective-permute-start(f32[544,128]{1,0:T(8,128)S(1)} %dynamic-slice_bitcast_fusion), channel_id=1, source_target_pairs={{0,1},{1,0},{2,3},{3,2},{4,5},{5,4},{6,7},{7,6},{8,9},{9,8},{10,11... | collective-permute-start | bytes 835592 | tf_op jit(solution)/shard_map/ppermute | solution.py:38
  33.6 4.8 %collective-permute-start.8 = (f32[136,128]{1,0:T(8,128)S(1)}, f32[136,128]{1,0:T(8,128)S(1)}, u32[]{:S(2)}, u32[]{:S(2)}) collective-permute-start(f32[136,128]{1,0:T(8,128)S(1)} %get-tuple-element.25), channel_id=1, source_target_pairs={{0,8},{8,0},{16,24},{24,16},{1,9},{9,1},{17,25},{25,17},{2,10},{10... | collective-permute-start | bytes 208904 | tf_op jit(solution)/shard_map/ppermute | solution.py:38
  34.2 5.4 %collective-permute-start.10 = (f32[136,128]{1,0:T(8,128)S(1)}, f32[136,128]{1,0:T(8,128)S(1)}, u32[]{:S(2)}, u32[]{:S(2)}) collective-permute-start(f32[136,128]{1,0:T(8,128)S(1)} %get-tuple-element.26), channel_id=1, source_target_pairs={{0,24},{8,16},{16,8},{24,0},{1,25},{9,17},{17,9},{25,1},{2,26},{10... | collective-permute-start | bytes 208904 | tf_op jit(solution)/shard_map/ppermute | solution.py:38
  35.8 5.0 %collective-permute-start.9 = (f32[136,128]{1,0:T(8,128)S(1)}, f32[136,128]{1,0:T(8,128)S(1)}, u32[]{:S(2)}, u32[]{:S(2)}) collective-permute-start(f32[136,128]{1,0:T(8,128)S(1)} %get-tuple-element.27), channel_id=1, source_target_pairs={{0,16},{8,24},{16,0},{24,8},{1,17},{9,25},{17,1},{25,9},{2,18},{10... | collective-permute-start | bytes 208904 | tf_op jit(solution)/shard_map/ppermute | solution.py:38
  40.8 6.8 %collective-permute-start.13 = (f32[136,128]{1,0:T(8,128)S(1)}, f32[136,128]{1,0:T(8,128)S(1)}, u32[]{:S(2)}, u32[]{:S(2)}) collective-permute-start(f32[136,128]{1,0:T(8,128)S(1)} %fusion.1), channel_id=1, source_target_pairs={{0,6},{1,7},{2,4},{3,5},{4,2},{5,3},{6,0},{7,1},{8,14},{9,15},{10,... | collective-permute-start | bytes 208904 | tf_op jit(solution)/shard_map/ppermute | solution.py:38
  44.5 5.8 %collective-permute-start.12 = (f32[136,128]{1,0:T(8,128)S(1)}, f32[136,128]{1,0:T(8,128)S(1)}, u32[]{:S(2)}, u32[]{:S(2)}) collective-permute-start(f32[136,128]{1,0:T(8,128)S(1)} %fusion.1), channel_id=1, source_target_pairs={{0,4},{1,5},{2,6},{3,7},{4,0},{5,1},{6,2},{7,3},{8,12},{9,13},{10,... | collective-permute-start | bytes 208904 | tf_op jit(solution)/shard_map/ppermute | solution.py:38
  44.5 5.8 %collective-permute-start.11 = (f32[136,128]{1,0:T(8,128)S(1)}, f32[136,128]{1,0:T(8,128)S(1)}, u32[]{:S(2)}, u32[]{:S(2)}) collective-permute-start(f32[136,128]{1,0:T(8,128)S(1)} %fusion.1), channel_id=1, source_target_pairs={{0,2},{1,3},{2,0},{3,1},{4,6},{5,7},{6,4},{7,5},{8,10},{9,11},{10,... | collective-permute-start | bytes 208904 | tf_op jit(solution)/shard_map/ppermute | solution.py:38
  50.2 5.7 %collective-permute-start.16 = (f32[136,128]{1,0:T(8,128)S(1)}, f32[136,128]{1,0:T(8,128)S(1)}, u32[]{:S(2)}, u32[]{:S(2)}) collective-permute-start(f32[136,128]{1,0:T(8,128)S(1)} %add_add_fusion), channel_id=1, source_target_pairs={{0,24},{8,16},{16,8},{24,0},{1,25},{9,17},{17,9},{25,1},{2,26},{10... | collective-permute-start | bytes 208904 | tf_op jit(solution)/shard_map/ppermute | solution.py:38
  51.9 4.7 %collective-permute-start.15 = (f32[136,128]{1,0:T(8,128)S(1)}, f32[136,128]{1,0:T(8,128)S(1)}, u32[]{:S(2)}, u32[]{:S(2)}) collective-permute-start(f32[136,128]{1,0:T(8,128)S(1)} %add_add_fusion), channel_id=1, source_target_pairs={{0,16},{8,24},{16,0},{24,8},{1,17},{9,25},{17,1},{25,9},{2,18},{10... | collective-permute-start | bytes 208904 | tf_op jit(solution)/shard_map/ppermute | solution.py:38
  53.2 4.3 %collective-permute-start.14 = (f32[136,128]{1,0:T(8,128)S(1)}, f32[136,128]{1,0:T(8,128)S(1)}, u32[]{:S(2)}, u32[]{:S(2)}) collective-permute-start(f32[136,128]{1,0:T(8,128)S(1)} %add_add_fusion), channel_id=1, source_target_pairs={{0,8},{8,0},{16,24},{24,16},{1,9},{9,1},{17,25},{25,17},{2,10},{10... | collective-permute-start | bytes 208904 | tf_op jit(solution)/shard_map/ppermute | solution.py:38
  57.7 4.6 %collective-permute-start.17 = (f32[544,128]{1,0:T(8,128)S(1)}, f32[544,128]{1,0:T(8,128)S(1)}, u32[]{:S(2)}, u32[]{:S(2)}) collective-permute-start(f32[544,128]{1,0:T(8,128)S(1)} %pad_maximum_fusion.4), channel_id=1, source_target_pairs={{0,1},{1,0},{2,3},{3,2},{4,5},{5,4},{6,7},{7,6},{8,9},{9,8},{10,11... | collective-permute-start | bytes 835592 | tf_op jit(solution)/shard_map/ppermute | solution.py:38
